TPU v7x, 1024 devices: a whole 8x8x8 slice. The times are simulated.
1024 devices in a mesh: dp: 16 (over z, core), expert: 64 (over y, x).
Axes of the slice: x: 8, y: 8, z: 8, core: 2. Of those that a mesh axis runs over, the one named last changes fastest.
Arguments:
- tokens: bfloat16 [131072, 3584], P(('dp', 'expert')), may hold values from -6 to 6
- expert_ids: int32 [131072, 1], P(('dp', 'expert')), may hold values from 0 to 63; in each aligned block of 128 rows (0 to 127, 128 to 255, ...) at most 4 rows name the same one
- gates: bfloat16 [131072], P(('dp', 'expert')), may hold values from 0.19921875 to 1
- cotangent: bfloat16 [131072, 1024], P(('dp', 'expert')), may hold values from -6 to 6
- weights: bfloat16 [64, 3584, 1024], P('expert'), may hold values from -0.09375 to 0.09375
Outputs:
- hidden: bfloat16 [131072, 1024], P(('dp', 'expert'))
- grad: float32 [64, 3584, 1024], P('expert', 'dp')
Inputs may be any that keep to these rules, and one draw needn't show every extreme that they name: `expert_ids`: among the 128 tokens of one device at most 4 name one expert; some device and expert reach 4 in every draw.
All inputs are finite; a program needn't handle non-finite values.
Results may differ from a plain program's by a relative error of at most 0.0029.
Values may be sent and summed in bfloat16 or wider, within the bound.
A program may use at most 64 MiB of HBM per device.

v0:
```python
import jax
import jax.numpy as jnp
from jax import lax
from jax.sharding import PartitionSpec as P


def on_device(tokens, expert_ids, gates, cotangent, weights):
    experts = lax.axis_size("expert")
    tok_count = tokens.shape[0]
    slots = max(2, 2 * tok_count // experts)
    ids = expert_ids[:, 0]
    onehot = (ids[:, None] == jnp.arange(experts, dtype=jnp.int32)[None, :]).astype(jnp.int32)
    before = jnp.cumsum(onehot, axis=0) - onehot
    rank = jnp.sum(before * onehot, axis=1)
    slot_of = ids * slots + rank
    placing = (jnp.arange(experts * slots, dtype=jnp.int32)[:, None] == slot_of[None, :]).astype(
        jnp.bfloat16
    )
    width = tokens.shape[1]
    inner = cotangent.shape[1]
    x_slots = (
        jnp.dot(placing, tokens, preferred_element_type=jnp.float32)
        .astype(jnp.bfloat16)
        .reshape(experts, slots, width)
    )
    c_slots = (
        jnp.dot(placing, cotangent, preferred_element_type=jnp.float32)
        .astype(jnp.bfloat16)
        .reshape(experts, slots, inner)
    )
    g_slots = (
        jnp.dot(placing, gates[:, None], preferred_element_type=jnp.float32)
        .astype(jnp.bfloat16)
        .reshape(experts, slots)
    )
    rows, cots, gvals = (
        lax.all_to_all(x_slots, "expert", split_axis=0, concat_axis=0, tiled=True),
        lax.all_to_all(c_slots, "expert", split_axis=0, concat_axis=0, tiled=True),
        lax.all_to_all(g_slots, "expert", split_axis=0, concat_axis=0, tiled=True),
    )
    row_count = experts * slots
    rows = rows.reshape(row_count, width)
    cots = cots.reshape(row_count, inner).astype(jnp.float32)
    gate = gvals.reshape(row_count, 1).astype(jnp.float32)
    pre = jnp.dot(rows, weights[0], preferred_element_type=jnp.float32)
    sig = jax.nn.sigmoid(pre)
    hval = (gate * pre * sig).astype(jnp.bfloat16).reshape(experts, slots, inner)
    returned = lax.all_to_all(hval, "expert", split_axis=0, concat_axis=0, tiled=True).reshape(
        row_count, inner
    )
    hidden = lax.dot_general(
        placing, returned, (((0,), (0,)), ((), ())), preferred_element_type=jnp.float32
    ).astype(jnp.bfloat16)
    dpre = (cots * gate * sig * (1.0 + pre * (1.0 - sig))).astype(jnp.bfloat16)
    grad = lax.psum_scatter(
        lax.dot_general(rows, dpre, (((0,), (0,)), ((), ())), preferred_element_type=jnp.float32),
        "dp",
        scatter_dimension=0,
        tiled=True,
    )
    return (hidden, grad[None])


def solution(mesh):
    return jax.shard_map(
        on_device,
        mesh=mesh,
        in_specs=(
            P(("dp", "expert"), None),
            P(("dp", "expert"), None),
            P(("dp", "expert")),
            P(("dp", "expert"), None),
            P("expert", None, None),
        ),
        out_specs=(P(("dp", "expert"), None), P("expert", "dp", None)),
        check_vma=False,
    )
```

profile of v0, /device:TPU:1, one launch (start us, length us, event | category | flops | bytes accessed | tf_op | source)
XLA Modules:
  0.0 233.1 jit_solution(10913052927578240948)
XLA Ops:
  7.2 0.0 copy-start
  7.2 0.8 fusion.10
  8.0 0.2 reduce_window_sum.11
  8.2 0.8 select_reduce_fusion
  9.0 0.7 multiply_add_fusion
  9.7 0.8 fusion.5
  10.5 0.8 all_to_all.20
  11.2 14.0 %all-to-all-start = ((bf16[64,1,4]{2,1,0:T(2,128)(2,1)}), bf16[64,1,4]{2,1,0:T(2,128)(2,1)S(1)}, u32[]{:S(2)}, u32[]{:S(2)}) async-start(bf16[64,1,4]{2,1,0:T(2,128)(2,1)} %all_to_all.20), calls=%async_computation | async-start | bytes 65536 | tf_op jit(solution)/shard_map/all_to_all | solution.py:39
  25.3 1.2 convolution_convert_fusion.1
  26.5 1.0 reshape.54
  27.5 8.6 %all-to-all-done = bf16[64,1,4]{2,1,0:T(2,128)(2,1)S(1)} async-done(((bf16[64,1,4]{2,1,0:T(2,128)(2,1)}), bf16[64,1,4]{2,1,0:T(2,128)(2,1)S(1)}, u32[]{:S(2)}, u32[]{:S(2)}) %all-to-all-start) | async-done | bytes 544 | tf_op jit(solution)/shard_map/all_to_all | solution.py:39
  36.1 4.6 %all-to-all-start.3 = ((bf16[64,4,1024]{2,1,0:T(4,128)(2,1)}), bf16[64,4,1024]{2,1,0:T(4,128)(2,1)S(1)}, u32[]{:S(2)}, u32[]{:S(2)}) async-start(bf16[64,4,1024]{2,1,0:T(4,128)(2,1)} %reshape.54), calls=%async_computation.3 | async-start | bytes 1048576 | tf_op jit(solution)/shard_map/all_to_all | solution.py:38
  40.7 0.0 copy-done
  40.7 0.6 convolution_convert_fusion
  41.3 1.5 reshape.50
  42.8 12.4 %all-to-all-done.3 = bf16[64,4,1024]{2,1,0:T(4,128)(2,1)S(1)} async-done(((bf16[64,4,1024]{2,1,0:T(4,128)(2,1)}), bf16[64,4,1024]{2,1,0:T(4,128)(2,1)S(1)}, u32[]{:S(2)}, u32[]{:S(2)}) %all-to-all-start.3) | async-done | bytes 524320 | tf_op jit(solution)/shard_map/all_to_all | solution.py:38
  55.2 5.5 %all-to-all-start.1 = ((bf16[64,4,3584]{2,1,0:T(4,128)(2,1)}), bf16[64,4,3584]{2,1,0:T(4,128)(2,1)}, u32[]{:S(2)}, u32[]{:S(2)}) async-start(bf16[64,4,3584]{2,1,0:T(4,128)(2,1)} %reshape.50), calls=%async_computation.1 | async-start | bytes 3670016 | tf_op jit(solution)/shard_map/all_to_all | solution.py:37
  60.7 0.0 reduce-scatter.2.cloned.1.call-start
  60.8 0.1 convert_reduce_fusion
  60.9 0.1 reshape.55
  61.0 1.0 reshape.56
  62.0 37.3 %all-to-all-done.1 = bf16[64,4,3584]{2,1,0:T(4,128)(2,1)} async-done(((bf16[64,4,3584]{2,1,0:T(4,128)(2,1)}), bf16[64,4,3584]{2,1,0:T(4,128)(2,1)}, u32[]{:S(2)}, u32[]{:S(2)}) %all-to-all-start.1) | async-done | bytes 1835040 | tf_op jit(solution)/shard_map/all_to_all | solution.py:37
  99.3 2.9 %reshape.51 = bf16[256,3584]{1,0:T(8,128)(2,1)S(1)} reshape(bf16[64,4,3584]{2,1,0:T(4,128)(2,1)} %all-to-all-done.1) | data formatting | bytes 3670016 | tf_op jit(solution)/shard_map/reshape | solution.py:42
  102.3 0.0 copy-start.1
  102.3 5.4 %multiply_convert_fusion.1 = (bf16[256,1024]{1,0:T(8,128)(2,1)S(1)}, f32[256,1024]{1,0:T(8,128)S(1)}) fusion(f32[256]{0:T(256)S(1)} %reshape.55, bf16[256,3584]{1,0:T(8,128)(2,1)S(1)} %reshape.51, bf16[1,3584,1024]{2,1,0:T(8,128)(2,1)} %param.9), kind=kOutput, calls=%fused_computation.6 | convolution fusion | flops 1880621056 | bytes 10748928 | tf_op jit(solution)/shard_map/dot_general | solution.py:45
  107.7 0.0 copy-done.1
  107.7 7.6 %fusion.2 = f32[3584,1024]{1,0:T(8,128)} fusion(bf16[256,3584]{1,0:T(8,128)(2,1)S(1)} %reshape.51, f32[256,1024]{1,0:T(8,128)S(1)} %get-tuple-element.3, f32[256,1024]{1,0:T(8,128)S(1)} %copy-done.1, f32[256]{0:T(256)S(1)} %reshape.55), kind=kOutput, calls=%fused_computation.8 | convolution fusion | flops 1881669632 | bytes 18613248 | tf_op jit(solution)/shard_map/dot_general | solution.py:56
  115.3 0.0 reduce-scatter.2.cloned.1.call-update
  115.3 0.2 reshape.52
  115.5 30.8 %all_to_all.25 = bf16[64,4,1024]{2,1,0:T(4,128)(2,1)S(1)} all-to-all(bf16[64,4,1024]{2,1,0:T(4,128)(2,1)S(1)} %reshape.52), channel_id=1, replica_groups=mesh['dp'=16,'expert'=64] {'expert'}, dimensions={0} | all-to-all | bytes 1048576 | tf_op jit(solution)/shard_map/all_to_all | solution.py:48
  146.3 0.1 reshape.53
  146.4 1.0 convolution_convert_fusion.2
  147.4 78.9 %reduce-scatter.2.cloned.1.call-done = f32[224,1024]{1,0:T(8,128)} async-done(((f32[3584,1024]{1,0:T(8,128)}), f32[224,1024]{1,0:T(8,128)}) %reduce-scatter.2.cloned.1.call-update) | async-done | bytes 917520 | tf_op jit(solution)/shard_map/reduce_scatter | solution.py:55
  (1 shorter events, 0.0 us)
Async XLA Ops:
  7.2 33.5 %copy-start = (bf16[128,3584]{1,0:T(8,128)(2,1)S(1)}, bf16[128,3584]{1,0:T(8,128)(2,1)}, u32[]{:S(2)}) copy-start(bf16[128,3584]{1,0:T(8,128)(2,1)} %param.5) | copy-start | bytes 2752516
  11.2 24.8 %all-to-all-start = ((bf16[64,1,4]{2,1,0:T(2,128)(2,1)}), bf16[64,1,4]{2,1,0:T(2,128)(2,1)S(1)}, u32[]{:S(2)}, u32[]{:S(2)}) async-start(bf16[64,1,4]{2,1,0:T(2,128)(2,1)} %all_to_all.20), calls=%async_computation | async-start | bytes 65536 | tf_op jit(solution)/shard_map/all_to_all | solution.py:39
  36.1 19.1 %all-to-all-start.3 = ((bf16[64,4,1024]{2,1,0:T(4,128)(2,1)}), bf16[64,4,1024]{2,1,0:T(4,128)(2,1)S(1)}, u32[]{:S(2)}, u32[]{:S(2)}) async-start(bf16[64,4,1024]{2,1,0:T(4,128)(2,1)} %reshape.54), calls=%async_computation.3 | async-start | bytes 1048576 | tf_op jit(solution)/shard_map/all_to_all | solution.py:38
  55.2 44.2 %all-to-all-start.1 = ((bf16[64,4,3584]{2,1,0:T(4,128)(2,1)}), bf16[64,4,3584]{2,1,0:T(4,128)(2,1)}, u32[]{:S(2)}, u32[]{:S(2)}) async-start(bf16[64,4,3584]{2,1,0:T(4,128)(2,1)} %reshape.50), calls=%async_computation.1 | async-start | bytes 3670016 | tf_op jit(solution)/shard_map/all_to_all | solution.py:37
  60.7 165.6 %reduce-scatter.2.cloned.1.call-start = ((), (), s32[]{:S(2)}) async-start(), calls=%async_computation.5 | async-start | bytes 15597568 | tf_op jit(solution)/shard_map/reduce_scatter | solution.py:55
  102.3 5.4 %copy-start.1 = (f32[256,1024]{1,0:T(8,128)S(1)}, f32[256,1024]{1,0:T(8,128)}, u32[]{:S(2)}) copy-start(f32[256,1024]{1,0:T(8,128)} %reshape.56) | copy-start | bytes 3145732
Sparse Core Ops, SparseCore 0:
  115.4 110.8 reduce-scatter.1
where the time goes:
time: 235 us; the launch traced here: 233 us
  waiting for transfers between devices  137 us (58%)
  blocking collectives  30.8 us (13%)
  starting transfers between devices  24.2 us (10%)
  matrix products  16.6 us (7%)
  between operations  14.1 us (6%)
  local copies, waits for them, and re-layouts  7.61 us (3%)
  other arithmetic  2.58 us (1%)
    reduce_scatter x1, waiting for transfers between devices, on_device(): lax.psum_scatter(lax.dot_general(rows, dpre, (((0,), (0,)), ((), ())), pr...  78.9 us
    all_to_all x1, waiting for transfers between devices, on_device(): lax.all_to_all(x_slots, 'expert', split_axis=0, concat_axis=0, tiled=True)  37.3 us
    all_to_all x1, blocking collectives, on_device(): lax.all_to_all(hval, 'expert', split_axis=0, concat_axis=0, tiled=True)  30.8 us
    all_to_all x1, starting transfers between devices, on_device(): lax.all_to_all(g_slots, 'expert', split_axis=0, concat_axis=0, tiled=True)  14 us
    all_to_all x1, waiting for transfers between devices, on_device(): lax.all_to_all(c_slots, 'expert', split_axis=0, concat_axis=0, tiled=True)  12.4 us
    all_to_all x1, waiting for transfers between devices, on_device(): lax.all_to_all(g_slots, 'expert', split_axis=0, concat_axis=0, tiled=True)  8.56 us
    dot_general x1, matrix products, on_device(): lax.dot_general(rows, dpre, (((0,), (0,)), ((), ())), preferred_element_t...  7.6 us
    all_to_all x1, starting transfers between devices, on_device(): lax.all_to_all(x_slots, 'expert', split_axis=0, concat_axis=0, tiled=True)  5.53 us
  transfers between devices with their start and end apart: 4, of which 4 were waited for; matrix products, arithmetic and copies ran while one was open for 3% of the time, Pallas kernels for 0%

commit v1 on v0

v1 whole, which is shorter than its diff:
```python
import functools

import jax
import jax.numpy as jnp
from jax import lax
from jax.experimental import pallas as pl
from jax.experimental.pallas import tpu as pltpu
from jax.sharding import PartitionSpec as P

MESH = pl.DeviceIdType.MESH
LANES = 128
BF = jnp.bfloat16
F32 = jnp.float32


def aligned(start, size):
    return pl.ds(pl.multiple_of(start, size), size)


def kernel(
    cfg,
    ids_ref,
    gates_ref,
    tok_hbm,
    cot_hbm,
    w_hbm,
    hid_ref,
    grad_ref,
    tok,
    cot,
    w,
    xs,
    cs,
    xr,
    cr,
    xt,
    xtp,
    fac,
    dpre,
    dprep,
    hv,
    hr,
    sbuf,
    rbuf,
    spare,
    local_sem,
    x_sem,
    c_sem,
    h_sem,
    t_sem,
    d_sem,
    rs_send,
    rs_recv,
):
    experts, cap, side, ring = cfg
    rows = experts * cap
    tall = experts // side
    width, inner = w.shape
    count = tok.shape[0]
    share = grad_ref.shape[0]
    half = share // 2
    far = ring // 2
    steps = ring - 1

    dp = lax.axis_index("dp")
    me = lax.axis_index("expert")
    z, core = dp // 2, dp % 2
    my_y, my_x = me // side, me % side
    partner = 2 * z + 1 - core
    ahead = 2 * ((z + 1) % ring) + core
    behind = 2 * ((z + ring - 1) % ring) + core

    def zigzag(i, n):
        return jnp.where(i % 2 == 1, (i + 1) // 2, (n - i // 2) % n)

    def peer(k):
        py = (my_y + zigzag(k // side, tall)) % tall
        px = (my_x + zigzag(k % side, side)) % side
        return py * side + px

    load_tok = pltpu.make_async_copy(tok_hbm, tok, local_sem.at[0])
    load_cot = pltpu.make_async_copy(cot_hbm, cot, local_sem.at[1])
    load_w = pltpu.make_async_copy(w_hbm.at[0], w, local_sem.at[2])
    load_tok.start()
    load_cot.start()

    barrier = pltpu.get_barrier_semaphore()

    def greet(k, carry):
        pl.semaphore_signal(barrier, inc=1, device_id=(dp, peer(k)), device_id_type=MESH)
        return carry

    lax.fori_loop(1, experts, greet, 0)
    for other in (partner, ahead, behind):
        pl.semaphore_signal(barrier, inc=1, device_id=(other, me), device_id_type=MESH)
    load_w.start()

    mine = jnp.broadcast_to(ids_ref[...], (count, count))
    earlier = lax.broadcasted_iota(jnp.int32, (count, count), 0) < lax.broadcasted_iota(
        jnp.int32, (count, count), 1
    )
    same = jnp.where((mine == mine.T) & earlier, 1, 0)
    slot = ids_ref[...] * cap + jnp.sum(same, axis=0, keepdims=True)
    hot = lax.broadcasted_iota(jnp.int32, (rows, count), 0) == slot
    placing32 = jnp.where(hot, 1.0, 0.0).astype(F32)
    placing = placing32.astype(BF)
    gate_col = jnp.sum(placing32 * gates_ref[...].astype(F32), axis=1, keepdims=True)
    xs[:, width:] = jnp.broadcast_to(gate_col, (rows, LANES)).astype(BF)

    load_tok.wait()
    block = 512 if width % 512 == 0 else LANES

    def place_x(i, carry):
        cols = aligned(i * block, block)
        xs[:, cols] = jnp.dot(placing, tok[:, cols], preferred_element_type=F32).astype(BF)
        return carry

    lax.fori_loop(0, width // block, place_x, 0)
    pl.semaphore_wait(barrier, experts - 1 + 3)

    def send_all(src, dst, sem, n):
        def go(k, carry):
            to = peer(k)
            pltpu.make_async_remote_copy(
                src_ref=src.at[aligned(to * cap, cap)],
                dst_ref=dst.at[aligned(me * cap, cap)],
                send_sem=sem.at[0],
                recv_sem=sem.at[1],
                device_id=(dp, to),
                device_id_type=MESH,
            ).start()
            return carry

        lax.fori_loop(1, experts, go, 0)
        own = aligned(me * cap, cap)
        pltpu.make_async_copy(src.at[own], dst.at[own], sem.at[1]).start()
        pltpu.make_async_copy(src.at[own], spare.at[n, pl.ds(0, cap), pl.ds(0, src.shape[1])], sem.at[0]).start()

    def whole(src, dst, sem):
        return pltpu.make_async_remote_copy(
            src_ref=src,
            dst_ref=dst,
            send_sem=sem.at[0],
            recv_sem=sem.at[1],
            device_id=(dp, peer(1)),
            device_id_type=MESH,
        )

    send_all(xs, xr, x_sem, 0)
    load_cot.wait()
    cs[...] = jnp.dot(placing, cot[...], preferred_element_type=F32).astype(BF)
    send_all(cs, cr, c_sem, 1)

    load_w.wait()
    whole(xs, xr, x_sem).wait_recv()

    tb = 256 if width % 256 == 0 else LANES

    def turn(i, carry):
        cols = aligned(i * tb, tb)
        xt[cols, :] = xr[:, cols].T
        return carry

    lax.fori_loop(0, width // tb, turn, 0)
    swaps = []
    for j in range(ring):
        swap = pltpu.make_async_remote_copy(
            src_ref=xt.at[aligned((2 * j + 1 - core) * share, share)],
            dst_ref=xtp.at[pl.ds(j * share, share)],
            send_sem=t_sem.at[0, j],
            recv_sem=t_sem.at[1, j],
            device_id=(partner, me),
            device_id_type=MESH,
        )
        swap.start()
        swaps.append(swap)

    nb = min(256, inner)

    def forward(i, carry):
        cols = aligned(i * nb, nb)
        pre = jnp.dot(xr[:, :width], w[:, cols], preferred_element_type=F32)
        gate = jnp.concatenate([xr[:, width:].astype(F32)] * (nb // LANES), axis=1)
        sig = jax.nn.sigmoid(pre)
        hv[:, cols] = (gate * pre * sig).astype(BF)
        fac[:, cols] = gate * sig * (1.0 + pre * (1.0 - sig))
        return carry

    lax.fori_loop(0, inner // nb, forward, 0)
    send_all(hv, hr, h_sem, 2)

    whole(cs, cr, c_sem).wait_recv()

    def backward(i, carry):
        cols = aligned(i * nb, nb)
        dpre[:, cols] = (cr[:, cols].astype(F32) * fac[:, cols]).astype(BF)
        return carry

    lax.fori_loop(0, inner // nb, backward, 0)
    give = pltpu.make_async_remote_copy(
        src_ref=dpre,
        dst_ref=dprep,
        send_sem=d_sem.at[0],
        recv_sem=d_sem.at[1],
        device_id=(partner, me),
        device_id_type=MESH,
    )
    give.start()
    for swap in swaps:
        swap.wait_recv()
    give.wait_recv()

    def chunk(j, which):
        own = xt[aligned((2 * j + core) * share + which * half, half), :]
        other = xtp[aligned(j * share + which * half, half), :]
        return jnp.dot(own, dpre[...], preferred_element_type=F32) + jnp.dot(
            other, dprep[...], preferred_element_type=F32
        )

    def message(way, m):
        return pltpu.make_async_remote_copy(
            src_ref=sbuf.at[way, m],
            dst_ref=rbuf.at[way, m],
            send_sem=rs_send.at[way, m],
            recv_sem=rs_recv.at[way, m],
            device_id=(ahead if way == 0 else behind, me),
            device_id_type=MESH,
        )

    def target(way, m):
        dist = far - (m + 1) // 2
        return (z + dist) % ring if way == 0 else (z + ring - dist) % ring

    for m in range(2):
        for way in range(2):
            sbuf[way, m] = chunk(target(way, m), (m + way) % 2).astype(BF)
            message(way, m).start()

    def relay(m, carry):
        for way in range(2):
            term = chunk(target(way, m), (m + way) % 2)
            message(way, m - 2).wait_recv()
            sbuf[way, m] = (term + rbuf[way, m - 2].astype(F32)).astype(BF)
            message(way, m).start()
        return carry

    lax.fori_loop(2, steps, relay, 0)

    for which in range(2):
        grad_ref[pl.ds(which * half, half), :] = chunk(z, which)

    whole(hv, hr, h_sem).wait_recv()
    hid_ref[...] = lax.dot_general(
        placing, hr[...], (((0,), (0,)), ((), ())), preferred_element_type=F32
    ).astype(BF)

    for m in (steps - 2, steps - 1):
        for way in range(2):
            message(way, m).wait_recv()
            at = pl.ds((m + way) % 2 * half, half)
            grad_ref[at, :] += rbuf[way, m].astype(F32)

    whole(xs, xr, x_sem).wait_send()
    whole(cs, cr, c_sem).wait_send()
    whole(hv, hr, h_sem).wait_send()
    for swap in swaps:
        swap.wait_send()
    give.wait_send()

    def drain(m, carry):
        for way in range(2):
            message(way, m).wait_send()
        return carry

    lax.fori_loop(0, steps, drain, 0)


def solution(mesh):
    n_dp, experts = mesh.shape["dp"], mesh.shape["expert"]
    ring = n_dp // 2
    side = 1
    while (2 * side) * (2 * side) <= experts:
        side *= 2

    def on_device(tokens, expert_ids, gates, cotangent, weights):
        count, width = tokens.shape
        inner = cotangent.shape[1]
        cap = max(2, 2 * count // experts)
        rows = experts * cap
        share = width // n_dp
        steps = ring - 1
        vmem = pl.BlockSpec(memory_space=pltpu.VMEM)
        hbm = pl.BlockSpec(memory_space=pl.ANY)
        dma = pltpu.SemaphoreType.DMA
        hidden, grad = pl.pallas_call(
            functools.partial(kernel, (experts, cap, side, ring)),
            out_shape=(
                jax.ShapeDtypeStruct((count, inner), BF),
                jax.ShapeDtypeStruct((share, inner), F32),
            ),
            in_specs=[vmem, vmem, hbm, hbm, hbm],
            out_specs=(vmem, vmem),
            scratch_shapes=[
                pltpu.VMEM((count, width), BF),
                pltpu.VMEM((count, inner), BF),
                pltpu.VMEM((width, inner), BF),
                pltpu.VMEM((rows, width + LANES), BF),
                pltpu.VMEM((rows, inner), BF),
                pltpu.VMEM((rows, width + LANES), BF),
                pltpu.VMEM((rows, inner), BF),
                pltpu.VMEM((width, rows), BF),
                pltpu.VMEM((width // 2, rows), BF),
                pltpu.VMEM((rows, inner), F32),
                pltpu.VMEM((rows, inner), BF),
                pltpu.VMEM((rows, inner), BF),
                pltpu.VMEM((rows, inner), BF),
                pltpu.VMEM((rows, inner), BF),
                pltpu.VMEM((2, steps, share // 2, inner), BF),
                pltpu.VMEM((2, steps, share // 2, inner), BF),
                pltpu.VMEM((3, max(cap, 8), width + LANES), BF),
                dma((3,)),
                dma((2,)),
                dma((2,)),
                dma((2,)),
                dma((2, ring)),
                dma((2,)),
                dma((2, steps)),
                dma((2, steps)),
            ],
            compiler_params=pltpu.CompilerParams(
                collective_id=0, has_side_effects=True, vmem_limit_bytes=56 << 20
            ),
        )(expert_ids.reshape(1, count), gates.reshape(1, count), tokens, cotangent, weights)
        return hidden, grad[None]

    return jax.shard_map(
        on_device,
        mesh=mesh,
        in_specs=(
            P(("dp", "expert"), None),
            P(("dp", "expert"), None),
            P(("dp", "expert")),
            P(("dp", "expert"), None),
            P("expert", None, None),
        ),
        out_specs=(P(("dp", "expert"), None), P("expert", "dp", None)),
        check_vma=False,
    )
```

time: 235 us -> 165 us (0.70)
  the two profiles are of different devices: /device:TPU:1 before, /device:TPU:119 now
where the time goes in v1:
time: 165 us
  Pallas kernels  160 us (97%)
  local copies, waits for them, and re-layouts  3.87 us (2%)
    pallas_call x1, Pallas kernels, on_device(): pl.pallas_call(functools.partial(kernel, (experts, cap, side, ring)), out...  160 us
    unnamed x2, local copies, waits for them, and re-layouts  3.87 us

profile of v1, /device:TPU:119, one launch (start us, length us, event | category | flops | bytes accessed | tf_op | source)
XLA Modules:
  0.0 164.6 jit_solution(11803494908047300017)
XLA Ops:
  0.6 160.1 %shard_map.68 = (bf16[128,1024]{1,0:T(8,128)(2,1)}, f32[224,1024]{1,0:T(8,128)}) custom-call(s32[1,128]{1,0:T(1,128)} %bitcast.4, bf16[1,128]{1,0:T(2,128)(2,1)} %bitcast.5, bf16[128,3584]{1,0:T(8,128)(2,1)} %tok_hbm.1, bf16[128,1024]{1,0:T(8,128)(2,1)} %cot_hbm.1, bf16[1,3584,1024]{2,1,0:T(8,128)(2,1)} %w_hbm.1), custom_call_target="tpu_custom_call" | custom-call | tf_op jit(solution)/shard_map/pallas_call | solution.py:295
  160.7 1.7 %copy.9 = bf16[128,1024]{1,0:T(8,128)(2,1)} copy(bf16[128,1024]{1,0:T(8,128)(2,1)} %get-tuple-element.8) | data formatting | bytes 524288
  162.4 2.2 %copy.10 = f32[1,224,1024]{2,1,0:T(8,128)} copy(f32[1,224,1024]{2,1,0:T(8,128)} %bitcast.3) | data formatting | bytes 1835008

commit v2 on v1

v2 whole, which is shorter than its diff:
```python
import functools

import jax
import jax.numpy as jnp
from jax import lax
from jax.experimental import pallas as pl
from jax.experimental.pallas import tpu as pltpu
from jax.sharding import PartitionSpec as P

MESH = pl.DeviceIdType.MESH
LANES = 128
BF = jnp.bfloat16
F32 = jnp.float32


def aligned(start, size):
    return pl.ds(pl.multiple_of(start, size), size)


def kernel(
    cfg,
    ids_ref,
    gates_ref,
    tok_hbm,
    cot_hbm,
    w_hbm,
    hid_ref,
    grad_ref,
    tok,
    cot,
    w,
    first,
    middle,
    last,
    h_first,
    h_middle,
    h_last,
    xt,
    xtp,
    fac,
    dpre,
    dprep,
    sbuf,
    rbuf,
    local_sem,
    own_sem,
    hop_send,
    hop_recv,
    t_sem,
    d_sem,
    rs_send,
    rs_recv,
):
    cap, side, tall, ring, slices, pieces = cfg
    rows = tall * side * cap
    width, inner = w.shape
    count = tok.shape[0]
    share = grad_ref.shape[0]
    half = share // 2
    far = ring // 2
    steps = ring - 1
    part = inner // slices
    n_x = len(pieces) - slices

    dp = lax.axis_index("dp")
    me = lax.axis_index("expert")
    z, core = dp // 2, dp % 2
    my_y, my_x = me // side, me % side
    partner = 2 * z + 1 - core
    ahead = 2 * ((z + 1) % ring) + core
    behind = 2 * ((z + ring - 1) % ring) + core

    def zigzag(i, n):
        return jnp.where(i % 2 == 1, (i + 1) // 2, (n - i // 2) % n)

    def y_peer(k):
        return (my_y + zigzag(k, tall)) % tall

    def x_peer(k):
        return (my_x + zigzag(k, side)) % side

    load_tok = pltpu.make_async_copy(tok_hbm, tok, local_sem.at[0])
    load_cot = pltpu.make_async_copy(cot_hbm, cot, local_sem.at[1])
    load_w = pltpu.make_async_copy(w_hbm.at[0], w, local_sem.at[2])
    load_tok.start()
    load_cot.start()

    barrier = pltpu.get_barrier_semaphore()

    def greet(to_dp, to):
        pl.semaphore_signal(barrier, inc=1, device_id=(to_dp, to), device_id_type=MESH)

    def greet_y(k, carry):
        greet(dp, y_peer(k) * side + my_x)
        return carry

    def greet_x(k, carry):
        greet(dp, my_y * side + x_peer(k))
        return carry

    lax.fori_loop(1, tall, greet_y, 0)
    lax.fori_loop(1, side, greet_x, 0)
    for other in (partner, ahead, behind):
        greet(other, me)
    load_w.start()

    mine = jnp.broadcast_to(ids_ref[...], (count, count))
    earlier = lax.broadcasted_iota(jnp.int32, (count, count), 0) < lax.broadcasted_iota(
        jnp.int32, (count, count), 1
    )
    same = jnp.where((mine == mine.T) & earlier, 1, 0)
    slot = ids_ref[...] * cap + jnp.sum(same, axis=0, keepdims=True)
    hot = lax.broadcasted_iota(jnp.int32, (rows, count), 0) == slot
    placing32 = jnp.where(hot, 1.0, 0.0).astype(F32)
    placing = placing32.astype(BF)

    def folded(v):
        return v.reshape(tall, side * cap, v.shape[1])

    def flat(ref, start, size):
        return ref[:, :, start : start + size].reshape(rows, size)

    def placed(source, start, size):
        return folded(
            jnp.dot(placing, source[:, start : start + size], preferred_element_type=F32).astype(BF)
        )

    def place(p):
        start, size = pieces[p][0], pieces[p][1] + pieces[p][2]
        if p >= n_x:
            first[:, :, start : start + size] = placed(cot, start - width - LANES, size)
            return
        here = min(size, width - start)
        first[:, :, start : start + here] = placed(tok, start, here)
        if here < size:
            gate_col = jnp.sum(placing32 * gates_ref[...].astype(F32), axis=1, keepdims=True)
            first[:, :, width : width + LANES] = folded(
                jnp.broadcast_to(gate_col, (rows, LANES)).astype(BF)
            )

    def hop(src, dst, p, hopno, which, cols):
        def copy(s, d, to):
            pltpu.make_async_remote_copy(
                src_ref=s,
                dst_ref=d,
                send_sem=hop_send.at[p, hopno, which],
                recv_sem=hop_recv.at[p, hopno, which],
                device_id=(dp, to),
                device_id_type=MESH,
            ).start()

        if hopno == which:

            def go(k, carry):
                to = y_peer(k)
                copy(src.at[to, :, cols], dst.at[my_y, :, cols], to * side + my_x)
                return carry

            lax.fori_loop(1, tall, go, 0)
        else:
            mine4 = aligned(my_x * cap, cap)

            def go(k, carry):
                to = x_peer(k)
                copy(
                    src.at[:, aligned(to * cap, cap), cols],
                    dst.at[:, mine4, cols],
                    my_y * side + to,
                )
                return carry

            lax.fori_loop(1, side, go, 0)
        own_copy(src, dst, p, hopno, which, cols).start()

    def own_copy(src, dst, p, hopno, which, cols):
        if hopno == which:
            s, d = src.at[my_y, :, cols], dst.at[my_y, :, cols]
        else:
            mine4 = aligned(my_x * cap, cap)
            s, d = src.at[:, mine4, cols], dst.at[:, mine4, cols]
        return pltpu.make_async_copy(s, d, own_sem.at[p, hopno, which])

    def others(src, dst, p, hopno, which, cols):
        n = tall - 1 if hopno == which else tall * (side - 1) // side
        return pltpu.make_async_remote_copy(
            src_ref=src.at[pl.ds(0, n), :, cols],
            dst_ref=dst.at[pl.ds(0, n), :, cols],
            send_sem=hop_send.at[p, hopno, which],
            recv_sem=hop_recv.at[p, hopno, which],
            device_id=(ahead, me),
            device_id_type=MESH,
        )

    def bufs(p, hopno):
        chain = (first, middle, last) if p < len(pieces) else (h_first, h_middle, h_last)
        return chain[hopno], chain[hopno + 1]

    def blocks(p):
        start, a, b = pieces[p] if p < len(pieces) else (0, inner // 2, inner // 2)
        return ((0, pl.ds(start, a)), (1, pl.ds(start + a, b)))

    def send_piece(p, hopno):
        src, dst = bufs(p, hopno)
        for which, cols in blocks(p):
            hop(src, dst, p, hopno, which, cols)

    def await_piece(p, hopno):
        src, dst = bufs(p, hopno)
        for which, cols in blocks(p):
            own_copy(src, dst, p, hopno, which, cols).wait()
            others(src, dst, p, hopno, which, cols).wait_recv()

    nb = min(256, part)

    def swap(j):
        return pltpu.make_async_remote_copy(
            src_ref=xt.at[aligned((2 * j + 1 - core) * share, share)],
            dst_ref=xtp.at[pl.ds(j * share, share)],
            send_sem=t_sem.at[0, j],
            recv_sem=t_sem.at[1, j],
            device_id=(partner, me),
            device_id_type=MESH,
        )

    def forward(p):
        start = pieces[p][0]
        size = min(pieces[p][1] + pieces[p][2], width - start)
        tb = 256 if size % 256 == 0 else LANES
        for i in range(size // tb):
            at = start + i * tb
            xt[pl.ds(at, tb), :] = flat(last, at, tb).T
        if p == n_x - 1:
            for j in range(ring):
                swap(j).start()

        def one(i, carry):
            cols = aligned(i * nb, nb)
            pre = jnp.dot(
                flat(last, start, size), w[start : start + size, cols], preferred_element_type=F32
            )
            if p > 0:
                pre = pre + fac[:, cols]
            if p < n_x - 1:
                fac[:, cols] = pre
                return carry
            gate = jnp.concatenate([flat(last, width, LANES).astype(F32)] * (nb // LANES), axis=1)
            sig = jax.nn.sigmoid(pre)
            h_first[:, :, cols] = folded((gate * pre * sig).astype(BF))
            fac[:, cols] = gate * sig * (1.0 + pre * (1.0 - sig))
            return carry

        lax.fori_loop(0, inner // nb, one, 0)

    def give(hs):
        return pltpu.make_async_remote_copy(
            src_ref=dpre.at[hs],
            dst_ref=dprep.at[hs],
            send_sem=d_sem.at[0, hs],
            recv_sem=d_sem.at[1, hs],
            device_id=(partner, me),
            device_id_type=MESH,
        )

    def chunk(j, which, hs):
        own = xt[aligned((2 * j + core) * share + which * half, half), :]
        other = xtp[aligned(j * share + which * half, half), :]
        return jnp.dot(own, dpre[hs], preferred_element_type=F32) + jnp.dot(
            other, dprep[hs], preferred_element_type=F32
        )

    def message(way, hs, m):
        return pltpu.make_async_remote_copy(
            src_ref=sbuf.at[way, hs, m],
            dst_ref=rbuf.at[way, hs, m],
            send_sem=rs_send.at[way, hs, m],
            recv_sem=rs_recv.at[way, hs, m],
            device_id=(ahead if way == 0 else behind, me),
            device_id_type=MESH,
        )

    def target(way, m):
        dist = far - (m + 1) // 2
        return (z + dist) % ring if way == 0 else (z + ring - dist) % ring

    def backward(hs):
        for i in range(part // nb):
            at = hs * part + i * nb
            dpre[hs, :, i * nb : (i + 1) * nb] = (
                flat(last, width + LANES + at, nb).astype(F32) * fac[:, at : at + nb]
            ).astype(BF)
        give(hs).start()
        if hs == 0:
            for j in range(ring):
                swap(j).wait_recv()
        give(hs).wait_recv()
        for m in range(2):
            for way in range(2):
                sbuf[way, hs, m] = chunk(target(way, m), (m + way) % 2, hs).astype(BF)
                message(way, hs, m).start()

    load_tok.wait()
    place(0)
    pl.semaphore_wait(barrier, tall - 1 + side - 1 + 3)
    send_piece(0, 0)
    n_p = len(pieces)
    place(1)
    send_piece(1, 0)
    load_cot.wait()
    for p in range(2, n_p):
        place(p)
    load_w.wait()

    def work(p):
        await_piece(p, 1)
        if p < n_x:
            forward(p)
        else:
            backward(p - n_x)

    for p in range(n_p):
        await_piece(p, 0)
        send_piece(p, 1)
        if p + 2 < n_p:
            send_piece(p + 2, 0)
        if p == n_p - 1:
            send_piece(n_p, 0)
        if p > 0:
            work(p - 1)
    work(n_p - 1)

    def relay(m, carry):
        for hs in range(slices):
            for way in range(2):
                term = chunk(target(way, m), (m + way) % 2, hs)
                message(way, hs, m - 2).wait_recv()
                sbuf[way, hs, m] = (term + rbuf[way, hs, m - 2].astype(F32)).astype(BF)
                message(way, hs, m).start()
        return carry

    relay(2, 0)
    await_piece(n_p, 0)
    send_piece(n_p, 1)
    lax.fori_loop(3, steps, relay, 0)

    for which in range(2):
        for hs in range(slices):
            grad_ref[pl.ds(which * half, half), pl.ds(hs * part, part)] = chunk(z, which, hs)

    await_piece(n_p, 1)
    hid_ref[...] = lax.dot_general(
        placing, flat(h_last, 0, inner), (((0,), (0,)), ((), ())), preferred_element_type=F32
    ).astype(BF)

    for m in (steps - 2, steps - 1):
        for hs in range(slices):
            for way in range(2):
                message(way, hs, m).wait_recv()
                at = pl.ds((m + way) % 2 * half, half)
                grad_ref[at, pl.ds(hs * part, part)] += rbuf[way, hs, m].astype(F32)

    for p in range(n_p + 1):
        for hopno in range(2):
            src, dst = bufs(p, hopno)
            for which, cols in blocks(p):
                others(src, dst, p, hopno, which, cols).wait_send()
    for j in range(ring):
        swap(j).wait_send()
    for hs in range(slices):
        give(hs).wait_send()

    def drain(m, carry):
        for hs in range(slices):
            for way in range(2):
                message(way, hs, m).wait_send()
        return carry

    lax.fori_loop(0, steps, drain, 0)


def solution(mesh):
    n_dp, experts = mesh.shape["dp"], mesh.shape["expert"]
    ring = n_dp // 2
    side = 1
    while (2 * side) * (2 * side) <= experts:
        side *= 2
    tall = experts // side

    def on_device(tokens, expert_ids, gates, cotangent, weights):
        count, width = tokens.shape
        inner = cotangent.shape[1]
        cap = max(2, 2 * count // experts)
        rows = experts * cap
        share = width // n_dp
        steps = ring - 1
        slices = 2
        part = inner // slices
        pieces, at = [], 0
        while width - at >= 8 * LANES:
            pieces.append((at, 4 * LANES, 4 * LANES))
            at += 8 * LANES
        tiles = (width - at) // LANES + 1
        pieces.append((at, tiles // 2 * LANES, (tiles - tiles // 2) * LANES))
        for hs in range(slices):
            pieces.append((width + LANES + hs * part, part // 2, part // 2))
        cols = width + LANES + inner
        vmem = pl.BlockSpec(memory_space=pltpu.VMEM)
        hbm = pl.BlockSpec(memory_space=pl.ANY)
        dma = pltpu.SemaphoreType.DMA
        hidden, grad = pl.pallas_call(
            functools.partial(kernel, (cap, side, tall, ring, slices, tuple(pieces))),
            out_shape=(
                jax.ShapeDtypeStruct((count, inner), BF),
                jax.ShapeDtypeStruct((share, inner), F32),
            ),
            in_specs=[vmem, vmem, hbm, hbm, hbm],
            out_specs=(vmem, vmem),
            scratch_shapes=[
                pltpu.VMEM((count, width), BF),
                pltpu.VMEM((count, inner), BF),
                pltpu.VMEM((width, inner), BF),
                pltpu.VMEM((tall, side * cap, cols), BF),
                pltpu.VMEM((tall, side * cap, cols), BF),
                pltpu.VMEM((tall, side * cap, cols), BF),
                pltpu.VMEM((tall, side * cap, inner), BF),
                pltpu.VMEM((tall, side * cap, inner), BF),
                pltpu.VMEM((tall, side * cap, inner), BF),
                pltpu.VMEM((width, rows), BF),
                pltpu.VMEM((width // 2, rows), BF),
                pltpu.VMEM((rows, inner), F32),
                pltpu.VMEM((slices, rows, part), BF),
                pltpu.VMEM((slices, rows, part), BF),
                pltpu.VMEM((2, slices, steps, share // 2, part), BF),
                pltpu.VMEM((2, slices, steps, share // 2, part), BF),
                dma((3,)),
                dma((len(pieces) + 1, 2, 2)),
                dma((len(pieces) + 1, 2, 2)),
                dma((len(pieces) + 1, 2, 2)),
                dma((2, ring)),
                dma((2, slices)),
                dma((2, slices, steps)),
                dma((2, slices, steps)),
            ],
            compiler_params=pltpu.CompilerParams(
                collective_id=0, has_side_effects=True, vmem_limit_bytes=56 << 20
            ),
        )(expert_ids.reshape(1, count), gates.reshape(1, count), tokens, cotangent, weights)
        return hidden, grad[None]

    return jax.shard_map(
        on_device,
        mesh=mesh,
        in_specs=(
            P(("dp", "expert"), None),
            P(("dp", "expert"), None),
            P(("dp", "expert")),
            P(("dp", "expert"), None),
            P("expert", None, None),
        ),
        out_specs=(P(("dp", "expert"), None), P("expert", "dp", None)),
        check_vma=False,
    )
```

time: 165 us -> 124 us (0.75)
  the two profiles are of different devices: /device:TPU:119 before, /device:TPU:1 now
where the time goes in v2:
time: 124 us
  Pallas kernels  120 us (97%)
  local copies, waits for them, and re-layouts  3.87 us (3%)
    pallas_call x1, Pallas kernels, on_device(): pl.pallas_call(functools.partial(kernel, (cap, side, tall, ring, slices,...  120 us
    unnamed x2, local copies, waits for them, and re-layouts  3.87 us

profile of v2, /device:TPU:1, one launch (start us, length us, event | category | flops | bytes accessed | tf_op | source)
XLA Modules:
  0.0 124.0 jit_solution(4614872040186308289)
XLA Ops:
  0.6 119.5 %shard_map.68 = (bf16[128,1024]{1,0:T(8,128)(2,1)}, f32[224,1024]{1,0:T(8,128)}) custom-call(s32[1,128]{1,0:T(1,128)} %bitcast.4, bf16[1,128]{1,0:T(2,128)(2,1)} %bitcast.5, bf16[128,3584]{1,0:T(8,128)(2,1)} %tok_hbm.1, bf16[128,1024]{1,0:T(8,128)(2,1)} %cot_hbm.1, bf16[1,3584,1024]{2,1,0:T(8,128)(2,1)} %w_hbm.1), custom_call_target="tpu_custom_call" | custom-call | tf_op jit(solution)/shard_map/pallas_call | solution.py:409
  120.2 1.7 %copy.9 = bf16[128,1024]{1,0:T(8,128)(2,1)} copy(bf16[128,1024]{1,0:T(8,128)(2,1)} %get-tuple-element.8) | data formatting | bytes 524288
  121.8 2.2 %copy.10 = f32[1,224,1024]{2,1,0:T(8,128)} copy(f32[1,224,1024]{2,1,0:T(8,128)} %bitcast.3) | data formatting | bytes 1835008

commit v3 on v2

--- a/solution.py
+++ b/solution.py
@@ -19,13 +19,15 @@
 
 def kernel(
     cfg,
-    ids_ref,
-    gates_ref,
+    ids_hbm,
+    gates_hbm,
     tok_hbm,
     cot_hbm,
     w_hbm,
     hid_ref,
     grad_ref,
+    ids_ref,
+    gates_ref,
     tok,
     cot,
     w,
@@ -70,20 +72,22 @@
     ahead = 2 * ((z + 1) % ring) + core
     behind = 2 * ((z + ring - 1) % ring) + core
 
-    def zigzag(i, n):
-        return jnp.where(i % 2 == 1, (i + 1) // 2, (n - i // 2) % n)
+    def offset(i, n):
+        return jnp.where(i % 2 == 1, n - n // 2 - i // 2, n // 2 + i // 2)
 
     def y_peer(k):
-        return (my_y + zigzag(k, tall)) % tall
+        return (my_y + offset(k, tall)) % tall
 
     def x_peer(k):
-        return (my_x + zigzag(k, side)) % side
+        return (my_x + offset(k, side)) % side
 
     load_tok = pltpu.make_async_copy(tok_hbm, tok, local_sem.at[0])
     load_cot = pltpu.make_async_copy(cot_hbm, cot, local_sem.at[1])
     load_w = pltpu.make_async_copy(w_hbm.at[0], w, local_sem.at[2])
-    load_tok.start()
-    load_cot.start()
+    load_ids = pltpu.make_async_copy(ids_hbm, ids_ref, local_sem.at[3])
+    load_gates = pltpu.make_async_copy(gates_hbm, gates_ref, local_sem.at[4])
+    for load in (load_ids, load_gates, load_tok, load_cot):
+        load.start()
 
     barrier = pltpu.get_barrier_semaphore()
 
@@ -104,6 +108,8 @@
         greet(other, me)
     load_w.start()
 
+    load_ids.wait()
+    load_gates.wait()
     mine = jnp.broadcast_to(ids_ref[...], (count, count))
     earlier = lax.broadcasted_iota(jnp.int32, (count, count), 0) < lax.broadcasted_iota(
         jnp.int32, (count, count), 1
@@ -377,6 +383,17 @@
     lax.fori_loop(0, steps, drain, 0)
 
 
+def deliver(hid, grad, hid_out, grad_out, sem):
+    copies = [
+        pltpu.make_async_copy(hid, hid_out, sem.at[0]),
+        pltpu.make_async_copy(grad, grad_out, sem.at[1]),
+    ]
+    for copy in copies:
+        copy.start()
+    for copy in copies:
+        copy.wait()
+
+
 def solution(mesh):
     n_dp, experts = mesh.shape["dp"], mesh.shape["expert"]
     ring = n_dp // 2
@@ -392,7 +409,7 @@
         rows = experts * cap
         share = width // n_dp
         steps = ring - 1
-        slices = 2
+        slices = 4
         part = inner // slices
         pieces, at = [], 0
         while width - at >= 8 * LANES:
@@ -404,7 +421,8 @@
             pieces.append((width + LANES + hs * part, part // 2, part // 2))
         cols = width + LANES + inner
         vmem = pl.BlockSpec(memory_space=pltpu.VMEM)
-        hbm = pl.BlockSpec(memory_space=pl.ANY)
+        hbm = pl.BlockSpec(memory_space=pltpu.HBM)
+        anywhere = pl.BlockSpec(memory_space=pl.ANY)
         dma = pltpu.SemaphoreType.DMA
         hidden, grad = pl.pallas_call(
             functools.partial(kernel, (cap, side, tall, ring, slices, tuple(pieces))),
@@ -412,9 +430,11 @@
                 jax.ShapeDtypeStruct((count, inner), BF),
                 jax.ShapeDtypeStruct((share, inner), F32),
             ),
-            in_specs=[vmem, vmem, hbm, hbm, hbm],
+            in_specs=[hbm] * 5,
             out_specs=(vmem, vmem),
             scratch_shapes=[
+                pltpu.VMEM((1, count), jnp.int32),
+                pltpu.VMEM((1, count), BF),
                 pltpu.VMEM((count, width), BF),
                 pltpu.VMEM((count, inner), BF),
                 pltpu.VMEM((width, inner), BF),
@@ -431,7 +451,7 @@
                 pltpu.VMEM((slices, rows, part), BF),
                 pltpu.VMEM((2, slices, steps, share // 2, part), BF),
                 pltpu.VMEM((2, slices, steps, share // 2, part), BF),
-                dma((3,)),
+                dma((5,)),
                 dma((len(pieces) + 1, 2, 2)),
                 dma((len(pieces) + 1, 2, 2)),
                 dma((len(pieces) + 1, 2, 2)),
@@ -441,9 +461,31 @@
                 dma((2, slices, steps)),
             ],
             compiler_params=pltpu.CompilerParams(
-                collective_id=0, has_side_effects=True, vmem_limit_bytes=56 << 20
+                collective_id=0, has_side_effects=True, vmem_limit_bytes=44 << 20
             ),
-        )(expert_ids.reshape(1, count), gates.reshape(1, count), tokens, cotangent, weights)
+        )(
+            *[
+                pltpu.with_memory_space_constraint(v, pltpu.HBM)
+                for v in (
+                    expert_ids.reshape(1, count),
+                    gates.reshape(1, count),
+                    tokens,
+                    cotangent,
+                    weights,
+                )
+            ]
+        )
+        hidden, grad = pl.pallas_call(
+            deliver,
+            out_shape=(
+                jax.ShapeDtypeStruct(hidden.shape, hidden.dtype),
+                jax.ShapeDtypeStruct(grad.shape, grad.dtype),
+            ),
+            in_specs=[anywhere, anywhere],
+            out_specs=(hbm, hbm),
+            scratch_shapes=[dma((2,))],
+            compiler_params=pltpu.CompilerParams(vmem_limit_bytes=1 << 20),
+        )(hidden, grad)
         return hidden, grad[None]
 
     return jax.shard_map(

time: 124 us -> 117 us (0.944)
  Pallas kernels: 120 us -> 116 us
  local copies, waits for them, and re-layouts: 3.87 us -> 0 us
    pallas_call x1, Pallas kernels: 120 us -> 115 us  [on_device(): pl.pallas_call(functools.partial(kernel, (cap, side, tall, ring, slices,...]
    unnamed x2 -> x0, local copies, waits for them, and re-layouts: 3.87 us -> none
where the time goes in v3:
time: 117 us
  Pallas kernels  116 us (99%)
    pallas_call x1, Pallas kernels, on_device(): pl.pallas_call(functools.partial(kernel, (cap, side, tall, ring, slices,...  115 us

profile of v3, /device:TPU:1, one launch (start us, length us, event | category | flops | bytes accessed | tf_op | source)
XLA Modules:
  0.0 117.1 jit_solution(17945156937974555592)
XLA Ops:
  0.6 115.4 %shard_map.68 = (bf16[128,1024]{1,0:T(8,128)(2,1)S(1)}, f32[224,1024]{1,0:T(8,128)S(1)}) custom-call(s32[1,128]{1,0:T(1,128)} %bitcast.3, bf16[1,128]{1,0:T(2,128)(2,1)} %bitcast.4, bf16[128,3584]{1,0:T(8,128)(2,1)} %tok_hbm.1, bf16[128,1024]{1,0:T(8,128)(2,1)} %cot_hbm.1, bf16[1,3584,1024]{2,1,0:T(8,128)(2,1)} %w_hbm.1), custom_call_target="tpu_custom_call" | custom-call | tf_op jit(solution)/shard_map/pallas_call | solution.py:427
  116.0 1.0 shard_map.69
